TPU v7x, 256 devices: a whole 4x4x8 slice. The times are simulated.
256 devices in a mesh: inp: 32 (over y, z_hi, core), tm: 8 (over z_lo, x).
Axes of the slice: x: 4, y: 4, z: 8 (z_hi: 4, z_lo: 2; z = z_hi * 2 + z_lo), core: 2. Of those that a mesh axis runs over, the one named last changes fastest.
Arguments:
- voltages: bfloat16 [512, 524288], P('inp', 'tm'), may hold values from -6 to 6
- taps: float32 [4, 512], replicated, may hold values from -3 to 3
Outputs:
- visibility: float32 [256, 2, 512, 512], P(('inp', 'tm'))
All inputs are finite; a program needn't handle non-finite values.
Results may differ from a plain program's by a relative error of at most 0.0038.
Values may be sent and summed in bfloat16 or wider, within the bound.
A program may use at most 128 MiB of HBM per device.

v0:
```python
import math
import jax
import jax.numpy as jnp
from jax import lax
from jax.sharding import PartitionSpec as P


def from_behind(block, axis, distance):
    devices = range(lax.axis_size(axis))
    route = [(i - distance, i) for i in devices if i - distance in devices]
    return lax.ppermute(block, axis, route)


def grouped_table(width, per_device):
    sample_idx = lax.broadcasted_iota(jnp.int32, (width, width), 0)
    column = lax.broadcasted_iota(jnp.int32, (width, width), 1)
    group = column // (2 * per_device)
    plane = column % (2 * per_device) // per_device
    channel = group * per_device + column % per_device
    phase = sample_idx * channel % width
    angle = phase.astype(jnp.float32) * (2.0 * math.pi / width)
    cosine = jnp.cos(angle).astype(jnp.bfloat16)
    sine = (-jnp.sin(angle)).astype(jnp.bfloat16)
    return jnp.where(plane == 0, cosine, sine)


def correlate(real_part, imag_part, scale):
    stacked = jnp.concatenate([real_part, imag_part], axis=2)
    rotated = jnp.concatenate([imag_part, -real_part], axis=2)
    cross_real = jnp.einsum("rcs,qcs->crq", stacked, stacked, preferred_element_type=jnp.float32)
    cross_imag = jnp.einsum("rcs,qcs->crq", rotated, stacked, preferred_element_type=jnp.float32)
    return jnp.stack([cross_real, cross_imag], axis=1) * scale


def local(voltages, taps):
    inp_dev = voltages.shape[0]
    tap_count = taps.shape[0]
    width = taps.shape[1]
    spectra_count = voltages.shape[1] // width
    time_devices = lax.axis_size("tm")
    per_device = width // 2 // (lax.axis_size("inp") * time_devices)
    inputs_all = inp_dev * lax.axis_size("inp")
    scale = 1.0 / (spectra_count * time_devices * width)
    sample_blocks = voltages.reshape(inp_dev, spectra_count, width)
    history = from_behind(sample_blocks[:, spectra_count - (tap_count - 1) :, :], "tm", 1)
    padded = jnp.concatenate([history, sample_blocks], axis=1)
    filtered = jnp.zeros((inp_dev, spectra_count, width), jnp.float32)
    for tap in range(tap_count):
        filtered = filtered + taps[tap][None, None, :] * padded[
            :, tap : tap + spectra_count, :
        ].astype(jnp.float32)
    filtered = filtered.astype(jnp.bfloat16)
    table = grouped_table(width, per_device)
    spectra = jnp.einsum("isn,nj->ijs", filtered, table, preferred_element_type=jnp.float32).astype(
        jnp.bfloat16
    )
    turned = lax.all_to_all(
        lax.all_to_all(spectra, "inp", split_axis=1, concat_axis=0, tiled=True),
        "tm",
        split_axis=1,
        concat_axis=2,
        tiled=True,
    )
    planes = turned.reshape(inputs_all, 2, per_device, turned.shape[2])
    return correlate(planes[:, 0], planes[:, 1], scale)


def solution(mesh):
    in_specs = (P("inp", "tm"), P())
    out_specs = P(("inp", "tm"), None, None, None)
    return jax.shard_map(local, mesh=mesh, in_specs=in_specs, out_specs=out_specs, check_vma=False)
```

profile of v0, /device:TPU:1, one launch (start us, length us, event | category | flops | bytes accessed | tf_op | source)
XLA Modules:
  0.0 123.3 jit_solution(15991717198502754298)
XLA Ops:
  0.0 0.0 copy-start.2
  0.0 2.3 %copy.23 = bf16[2,8,128,512]{3,2,1,0:T(8,128)(2,1)S(1)} copy(bf16[2,8,128,512]{3,1,2,0:T(8,128)(2,1)} %bitcast.45) | data formatting | bytes 4194304
  2.3 3.9 %collective-permute-start = (bf16[16,3,512]{2,1,0:T(4,128)(2,1)S(1)}, bf16[16,3,512]{2,1,0:T(4,128)(2,1)S(1)}, u32[]{:S(2)}, u32[]{:S(2)}) collective-permute-start(bf16[16,3,512]{2,1,0:T(4,128)(2,1)S(1)} %slice.40), channel_id=1, source_target_pairs={{0,1},{1,2},{2,3},{3,4},{4,5},{5,6},{6,7},{8,9},{9,10},{10,11},{11... | collective-permute-start | bytes 147464 | tf_op jit(solution)/shard_map/ppermute | solution.py:11
  6.3 0.0 copy-done.2
  6.4 1.2 %collective-permute-done = bf16[16,3,512]{2,1,0:T(4,128)(2,1)S(1)} collective-permute-done((bf16[16,3,512]{2,1,0:T(4,128)(2,1)S(1)}, bf16[16,3,512]{2,1,0:T(4,128)(2,1)S(1)}, u32[]{:S(2)}, u32[]{:S(2)}) %collective-permute-start) | collective-permute-done | bytes 49184 | tf_op jit(solution)/shard_map/ppermute | solution.py:11
  7.6 7.0 %convert_bitcast_fusion = bf16[16,512,128]{2,1,0:T(8,128)(2,1)S(1)} fusion(bf16[16,128,512]{2,1,0:T(8,128)(2,1)S(1)} %bitcast.44, bf16[16,3,512]{2,1,0:T(4,128)(2,1)S(1)} %collective-permute-done, f32[512]{0:T(512)S(1)} %bitcast.48, f32[512]{0:T(512)S(1)} %bitcast.49, f32[512]{0:T(512)S(1)} %bitcast.47, f32[512]{0:T(512)S(1)} %bitcast.46, ...), kind=kOutput, calls=%fused_computation.12 | convolution fusion | flops 1102315520 | bytes 4260864 | tf_op jit(solution)/shard_map/isn,nj->ijs/dot_general | solution.py:54
  14.6 1.4 %copy.14 = bf16[16,512,128]{2,0,1:T(8,128)(2,1)S(1)} copy(bf16[16,512,128]{2,1,0:T(8,128)(2,1)S(1)} %convert_bitcast_fusion) | data formatting | bytes 4194304 | tf_op jit(solution)/shard_map/convert_element_type | solution.py:54
  16.0 54.6 %all_to_all.33 = bf16[16,512,128]{2,0,1:T(8,128)(2,1)S(1)} all-to-all(bf16[16,512,128]{2,0,1:T(8,128)(2,1)S(1)} %copy.14), channel_id=1, replica_groups=mesh['inp'=32,'tm'=8] {'inp'}, dimensions={1} | all-to-all | bytes 4194304 | tf_op jit(solution)/shard_map/all_to_all | solution.py:58
  70.5 0.5 copy.16
  71.1 0.5 copy.17
  71.6 40.8 %all_to_all.34 = bf16[512,16,128]{2,0,1:T(8,128)(2,1)} all-to-all(bf16[512,16,128]{2,0,1:T(8,128)(2,1)S(1)} %copy.17), channel_id=1, replica_groups=mesh['inp'=32,'tm'=8] {'tm'}, dimensions={1} | all-to-all | bytes 4194304 | tf_op jit(solution)/shard_map/all_to_all | solution.py:57
  112.4 2.9 %copy.18 = bf16[512,2,8,128]{0,3,2,1:T(8,128)(2,1)S(1)} copy(bf16[512,2,8,128]{3,0,1,2:T(8,128)(2,1)} %bitcast.41) | data formatting | bytes 4194304 | tf_op jit(solution)/shard_map/all_to_all | solution.py:57
  115.3 1.0 fusion.36
  116.3 1.1 slice_bitcast_fusion
  117.4 0.5 copy.19
  117.9 0.0 copy-start.1
  118.0 0.5 copy.20
  118.5 0.7 copy-done.1
  119.2 0.0 copy-start
  119.2 1.3 %convolution_bitcast_fusion = f32[1,1,512,512]{3,2,1,0:T(8,128)S(1)} fusion(bf16[512,1,1024]{0,2,1:T(8,128)(2,1)S(1)} %copy.20, bf16[512,1,1024]{0,2,1:T(8,128)(2,1)S(1)} %copy-done.1), kind=kOutput, calls=%fused_computation.18 | convolution fusion | flops 1077936128 | bytes 3145728 | tf_op jit(solution)/shard_map/rcs,qcs->crq/dot_general | solution.py:30
  120.4 0.0 copy-done
  120.5 1.3 %fusion.6 = f32[1,1,512,512]{3,2,1,0:T(8,128)S(1)} fusion(bf16[512,1,1024]{0,2,1:T(8,128)(2,1)S(1)} %copy-done, bf16[512,1,1024]{0,2,1:T(8,128)(2,1)S(1)} %copy.20, bf16[512,1,1024]{0,2,1:T(8,128)(2,1)S(1)} %copy-done.1), kind=kOutput, calls=%fused_computation.17 | convolution fusion | flops 1082130432 | bytes 4194304 | tf_op jit(solution)/shard_map/rcs,qcs->crq/dot_general | solution.py:31
  121.7 1.6 %maximum_multiply_fusion = f32[1,2,512,512]{3,2,1,0:T(8,128)} fusion(f32[1,1,512,512]{3,2,1,0:T(8,128)S(1)} %fusion.6, f32[1,1,512,512]{3,2,1,0:T(8,128)S(1)} %convolution_bitcast_fusion), kind=kLoop, calls=%fused_computation.11 | loop fusion | flops 1048576 | bytes 4194304 | tf_op jit(solution)/shard_map/mul | solution.py:32
  (5 shorter events, 0.1 us)
Async XLA Ops:
  0.0 6.3 %copy-start.2 = (f32[4,512]{1,0:T(4,128)S(1)}, f32[4,512]{1,0:T(4,128)}, u32[]{:S(2)}) copy-start(f32[4,512]{1,0:T(4,128)} %param.3) | copy-start | bytes 24580
  2.3 5.3 %collective-permute-start = (bf16[16,3,512]{2,1,0:T(4,128)(2,1)S(1)}, bf16[16,3,512]{2,1,0:T(4,128)(2,1)S(1)}, u32[]{:S(2)}, u32[]{:S(2)}) collective-permute-start(bf16[16,3,512]{2,1,0:T(4,128)(2,1)S(1)} %slice.40), channel_id=1, source_target_pairs={{0,1},{1,2},{2,3},{3,4},{4,5},{5,6},{6,7},{8,9},{9,10},{10,11},{11... | collective-permute-start | bytes 147464 | tf_op jit(solution)/shard_map/ppermute | solution.py:11
  117.9 1.2 copy-start.1
  119.2 1.3 %copy-start = (bf16[512,1,1024]{0,2,1:T(8,128)(2,1)S(1)}, bf16[512,1,1024]{0,2,1:T(8,128)(2,1)}, u32[]{:S(2)}) copy-start(bf16[512,1,1024]{0,2,1:T(8,128)(2,1)} %fusion.36) | copy-start | bytes 3145732
where the time goes:
time: 124 us; the launch traced here: 123 us
  blocking collectives  95.4 us (77%)
  local copies, waits for them, and re-layouts  10.5 us (8%)
  matrix products  9.53 us (8%)
  starting transfers between devices  3.95 us (3%)
  other arithmetic  2.61 us (2%)
  waiting for transfers between devices  1.25 us (1%)
    all_to_all x1, blocking collectives, local(): lax.all_to_all(spectra, 'inp', split_axis=1, concat_axis=0, tiled=True)  54.6 us
    all_to_all x1, blocking collectives, local(): lax.all_to_all(lax.all_to_all(spectra, 'inp', split_axis=1, concat_axis=0...  40.8 us
    dot_general x1, matrix products, local(): jnp.einsum('isn,nj->ijs', filtered, table, preferred_element_type=jnp.flo...  6.98 us
    ppermute x1, starting transfers between devices, from_behind(): return lax.ppermute(block, axis, route)  3.95 us
    unnamed x7, local copies, waits for them, and re-layouts  2.96 us
    all_to_all x1, local copies, waits for them, and re-layouts, local(): lax.all_to_all(lax.all_to_all(spectra, 'inp', split_axis=1, concat_axis=0...  2.85 us
  transfers between devices with their start and end apart: 1, of which 1 were waited for; matrix products, arithmetic and copies ran while one was open for 0% of the time, Pallas kernels for 0%

commit v1 on v0

--- a/solution.py
+++ b/solution.py
@@ -54,12 +54,20 @@
     spectra = jnp.einsum("isn,nj->ijs", filtered, table, preferred_element_type=jnp.float32).astype(
         jnp.bfloat16
     )
-    turned = lax.all_to_all(
-        lax.all_to_all(spectra, "inp", split_axis=1, concat_axis=0, tiled=True),
-        "tm",
-        split_axis=1,
-        concat_axis=2,
-        tiled=True,
+    turned = jnp.concatenate(
+        lax.all_to_all(
+            jnp.stack(
+                jnp.split(
+                    lax.all_to_all(spectra, "inp", split_axis=1, concat_axis=0, tiled=True),
+                    lax.axis_size("tm"),
+                    axis=1,
+                )
+            ),
+            "tm",
+            0,
+            0,
+        ),
+        axis=2,
     )
     planes = turned.reshape(inputs_all, 2, per_device, turned.shape[2])
     return correlate(planes[:, 0], planes[:, 1], scale)

time: 124 us -> 127 us (1.024)
  local copies, waits for them, and re-layouts: 10.5 us -> 14 us
    reshape x0 -> x1, local copies, waits for them, and re-layouts: none -> 4.72 us  [local(): jnp.concatenate(lax.all_to_all(jnp.stack(jnp.split(lax.all_to_all(spectra...]
    all_to_all x1 -> x0, local copies, waits for them, and re-layouts: 2.85 us -> none  [local(): lax.all_to_all(lax.all_to_all(spectra, 'inp', split_axis=1, concat_axis=0...]
    unnamed x7 -> x14, local copies, waits for them, and re-layouts: 2.96 us -> 4.82 us
where the time goes in v1:
time: 127 us
  blocking collectives  95.4 us (75%)
  local copies, waits for them, and re-layouts  14 us (11%)
  matrix products  9.53 us (8%)
  starting transfers between devices  3.95 us (3%)
  other arithmetic  2.61 us (2%)
    all_to_all x1, blocking collectives, local(): lax.all_to_all(spectra, 'inp', split_axis=1, concat_axis=0, tiled=True)  54.6 us
    all_to_all x1, blocking collectives, local(): lax.all_to_all(jnp.stack(jnp.split(lax.all_to_all(spectra, 'inp', split_a...  40.8 us
    dot_general x1, matrix products, local(): jnp.einsum('isn,nj->ijs', filtered, table, preferred_element_type=jnp.flo...  6.98 us
    unnamed x14, local copies, waits for them, and re-layouts  4.82 us
    reshape x1, local copies, waits for them, and re-layouts, local(): jnp.concatenate(lax.all_to_all(jnp.stack(jnp.split(lax.all_to_all(spectra...  4.72 us
    ppermute x1, starting transfers between devices, from_behind(): return lax.ppermute(block, axis, route)  3.95 us
  transfers between devices with their start and end apart: 1, of which 1 were waited for; matrix products, arithmetic and copies ran while one was open for 0% of the time, Pallas kernels for 0%

profile of v1, /device:TPU:1, one launch (start us, length us, event | category | flops | bytes accessed | tf_op | source)
XLA Modules:
  0.0 126.8 jit_solution(2474273075166737720)
XLA Ops:
  0.0 0.0 copy-start.2
  0.0 2.3 %copy.22 = bf16[2,8,128,512]{3,2,1,0:T(8,128)(2,1)S(1)} copy(bf16[2,8,128,512]{3,1,2,0:T(8,128)(2,1)} %bitcast.82) | data formatting | bytes 4194304
  2.3 3.9 %collective-permute-start = (bf16[16,3,512]{2,1,0:T(4,128)(2,1)S(1)}, bf16[16,3,512]{2,1,0:T(4,128)(2,1)S(1)}, u32[]{:S(2)}, u32[]{:S(2)}) collective-permute-start(bf16[16,3,512]{2,1,0:T(4,128)(2,1)S(1)} %slice.40), channel_id=1, source_target_pairs={{0,1},{1,2},{2,3},{3,4},{4,5},{5,6},{6,7},{8,9},{9,10},{10,11},{11... | collective-permute-start | bytes 147464 | tf_op jit(solution)/shard_map/ppermute | solution.py:11
  6.3 0.0 copy-done.2
  6.4 1.2 collective-permute-done
  7.6 7.0 %convert_bitcast_fusion = bf16[16,512,128]{2,1,0:T(8,128)(2,1)S(1)} fusion(bf16[16,128,512]{2,1,0:T(8,128)(2,1)S(1)} %bitcast.81, bf16[16,3,512]{2,1,0:T(4,128)(2,1)S(1)} %collective-permute-done, f32[512]{0:T(512)S(1)} %bitcast.85, f32[512]{0:T(512)S(1)} %bitcast.86, f32[512]{0:T(512)S(1)} %bitcast.84, f32[512]{0:T(512)S(1)} %bitcast.83, ...), kind=kOutput, calls=%fused_computation.12 | convolution fusion | flops 1102315520 | bytes 4260864 | tf_op jit(solution)/shard_map/isn,nj->ijs/dot_general | solution.py:54
  14.6 1.4 %copy.14 = bf16[16,512,128]{2,0,1:T(8,128)(2,1)S(1)} copy(bf16[16,512,128]{2,1,0:T(8,128)(2,1)S(1)} %convert_bitcast_fusion) | data formatting | bytes 4194304 | tf_op jit(solution)/shard_map/convert_element_type | solution.py:54
  16.0 54.6 %all_to_all.23 = bf16[16,512,128]{2,0,1:T(8,128)(2,1)S(1)} all-to-all(bf16[16,512,128]{2,0,1:T(8,128)(2,1)S(1)} %copy.14), channel_id=1, replica_groups=mesh['inp'=32,'tm'=8] {'inp'}, dimensions={1} | all-to-all | bytes 4194304 | tf_op jit(solution)/shard_map/all_to_all | solution.py:61
  70.5 0.5 copy.16
  71.1 0.1 fusion.30
  71.2 0.3 fusion.29
  71.5 0.3 fusion.28
  71.8 0.3 fusion.27
  72.1 0.2 fusion.26
  72.3 0.3 fusion.25
  72.6 0.3 fusion.24
  72.9 0.3 fusion.23
  73.2 40.8 %all_to_all.24 = bf16[8,512,2,128]{3,2,1,0:T(2,128)(2,1)} all-to-all(bf16[8,512,2,128]{3,2,1,0:T(2,128)(2,1)S(1)} %fusion.23), channel_id=1, replica_groups=mesh['inp'=32,'tm'=8] {'tm'}, dimensions={0} | all-to-all | bytes 4194304 | tf_op jit(solution)/shard_map/all_to_all | solution.py:58
  114.0 4.7 %copy.17 = bf16[512,2,8,128]{0,3,2,1:T(8,128)(2,1)S(1)} copy(bf16[512,2,8,128]{3,1,0,2:T(2,128)(2,1)} %bitcast.78) | data formatting | bytes 4194304 | tf_op jit(solution)/shard_map/reshape | solution.py:57
  118.8 1.0 fusion.44
  119.8 1.1 slice_bitcast_fusion
  120.9 0.5 copy.18
  121.4 0.0 copy-start.1
  121.4 0.5 copy.19
  122.0 0.7 copy-done.1
  122.7 0.0 copy-start
  122.7 1.3 %convolution_bitcast_fusion = f32[1,1,512,512]{3,2,1,0:T(8,128)S(1)} fusion(bf16[512,1,1024]{0,2,1:T(8,128)(2,1)S(1)} %copy.19, bf16[512,1,1024]{0,2,1:T(8,128)(2,1)S(1)} %copy-done.1), kind=kOutput, calls=%fused_computation.18 | convolution fusion | flops 1077936128 | bytes 3145728 | tf_op jit(solution)/shard_map/rcs,qcs->crq/dot_general | solution.py:30
  123.9 0.0 copy-done
  124.0 1.3 %fusion.6 = f32[1,1,512,512]{3,2,1,0:T(8,128)S(1)} fusion(bf16[512,1,1024]{0,2,1:T(8,128)(2,1)S(1)} %copy-done, bf16[512,1,1024]{0,2,1:T(8,128)(2,1)S(1)} %copy.19, bf16[512,1,1024]{0,2,1:T(8,128)(2,1)S(1)} %copy-done.1), kind=kOutput, calls=%fused_computation.17 | convolution fusion | flops 1082130432 | bytes 4194304 | tf_op jit(solution)/shard_map/rcs,qcs->crq/dot_general | solution.py:31
  125.2 1.6 %maximum_multiply_fusion = f32[1,2,512,512]{3,2,1,0:T(8,128)} fusion(f32[1,1,512,512]{3,2,1,0:T(8,128)S(1)} %fusion.6, f32[1,1,512,512]{3,2,1,0:T(8,128)S(1)} %convolution_bitcast_fusion), kind=kLoop, calls=%fused_computation.11 | loop fusion | flops 1048576 | bytes 4194304 | tf_op jit(solution)/shard_map/mul | solution.py:32
  (5 shorter events, 0.1 us)
Async XLA Ops:
  0.0 6.3 %copy-start.2 = (f32[4,512]{1,0:T(4,128)S(1)}, f32[4,512]{1,0:T(4,128)}, u32[]{:S(2)}) copy-start(f32[4,512]{1,0:T(4,128)} %param.3) | copy-start | bytes 24580
  2.3 5.3 %collective-permute-start = (bf16[16,3,512]{2,1,0:T(4,128)(2,1)S(1)}, bf16[16,3,512]{2,1,0:T(4,128)(2,1)S(1)}, u32[]{:S(2)}, u32[]{:S(2)}) collective-permute-start(bf16[16,3,512]{2,1,0:T(4,128)(2,1)S(1)} %slice.40), channel_id=1, source_target_pairs={{0,1},{1,2},{2,3},{3,4},{4,5},{5,6},{6,7},{8,9},{9,10},{10,11},{11... | collective-permute-start | bytes 147464 | tf_op jit(solution)/shard_map/ppermute | solution.py:11
  121.4 1.2 copy-start.1
  122.7 1.3 %copy-start = (bf16[512,1,1024]{0,2,1:T(8,128)(2,1)S(1)}, bf16[512,1,1024]{0,2,1:T(8,128)(2,1)}, u32[]{:S(2)}) copy-start(bf16[512,1,1024]{0,2,1:T(8,128)(2,1)} %fusion.44) | copy-start | bytes 3145732
